TPU v7x, 32 devices: a whole 2x2x4 slice. The times are simulated.
32 devices in a mesh: ctx: 16 (over z, y, core), head: 2 (over x).
Axes of the slice: x: 2, y: 2, z: 4, core: 2. Of those that a mesh axis runs over, the one named last changes fastest.
Arguments:
- queries: bfloat16 [4096, 4096], P(('ctx', 'head')), may hold values from -6 to 6
- keys: bfloat16 [4096, 1024], P(('ctx', 'head')), may hold values from -6 to 6
- values: bfloat16 [4096, 1024], P(('ctx', 'head')), may hold values from -6 to 6
- grad_out: bfloat16 [4096, 4096], P(('ctx', 'head')), may hold values from -6 to 6
- doc_ids: int32 [4096], replicated, may hold values from 0 to 3, never falling along the last dimension, each value on 1 to 2048 neighbouring positions
Outputs:
- attended: bfloat16 [4096, 4096], P(('ctx', 'head'))
- grad_queries: bfloat16 [4096, 4096], P(('ctx', 'head'))
- grad_keys: bfloat16 [4096, 1024], P(('ctx', 'head'))
- grad_values: bfloat16 [4096, 1024], P(('ctx', 'head'))
Inputs may be any that keep to these rules, and one draw needn't show every extreme that they name: `doc_ids`: document numbers never fall along the row; every document has 1 to 2048 tokens and one has exactly 2048.
All inputs are finite; a program needn't handle non-finite values.
Results may differ from a plain program's by a relative error of at most 0.023.
Values may be sent and summed in bfloat16 or wider, within the bound.
A program may use at most 64 MiB of HBM per device.

v0:
```python
import jax
import jax.numpy as jnp
from jax import lax
from jax.sharding import PartitionSpec as P

HD = 128
DOC_MOST = 2048


def shifted(value, axis, by):
    peers = lax.axis_size(axis)
    pairs = [(i, i + by) for i in range(peers) if 0 <= i + by < peers]
    return lax.ppermute(value, axis, pairs)


def per_device(queries, keys, values, grad_out, doc_ids):
    query_local, key_local, value_local, grad_local = (
        lax.all_to_all(queries, "head", split_axis=1, concat_axis=0, tiled=True),
        lax.all_to_all(keys, "head", split_axis=1, concat_axis=0, tiled=True),
        lax.all_to_all(values, "head", split_axis=1, concat_axis=0, tiled=True),
        lax.all_to_all(grad_out, "head", split_axis=1, concat_axis=0, tiled=True),
    )
    tok_rows = query_local.shape[0]
    kv_cols = key_local.shape[1]
    q_heads = query_local.shape[1] // HD
    kv_heads = kv_cols // HD
    group_size = q_heads // kv_heads
    distance = DOC_MOST // tok_rows
    blocks = distance + 1
    window = blocks * tok_rows
    softmax_scale = HD ** (-0.5)
    shard_index = lax.axis_index("ctx")
    paired = jnp.stack((key_local, value_local))
    key_band = jnp.zeros((2, blocks, tok_rows, kv_cols), jnp.bfloat16)
    key_band = key_band.at[:, 0].set(paired)

    def fetch_one(step_index, carried):
        moving, gathered = carried
        moving = shifted(moving, "ctx", 1)
        gathered = lax.dynamic_update_index_in_dim(gathered, moving, step_index, 1)
        return (moving, gathered)

    key_band = lax.fori_loop(1, blocks, fetch_one, (paired, key_band))[1]
    key_flat = key_band[0].reshape(window, kv_cols)
    value_flat = key_band[1].reshape(window, kv_cols)
    padded_docs = jnp.concatenate((jnp.full((DOC_MOST,), -1, jnp.int32), doc_ids), 0)
    ascending = lax.dynamic_slice_in_dim(padded_docs, shard_index * tok_rows, window, 0)
    doc_keys = ascending.reshape(blocks, tok_rows)[::-1].reshape(window)
    doc_rows = lax.dynamic_slice_in_dim(doc_ids, shard_index * tok_rows, tok_rows, 0)
    column_ids = jnp.arange(window, dtype=jnp.int32)
    block_ids = column_ids // tok_rows
    row_offset = column_ids % tok_rows
    row_ids = jnp.arange(tok_rows, dtype=jnp.int32)
    causal = (block_ids[None, :] > 0) | (row_offset[None, :] <= row_ids[:, None])
    visible = (doc_rows[:, None] == doc_keys[None, :]) & causal

    def one_head(head_index, carried):
        attended, grad_query, grad_key, grad_value, row_stats = carried
        kv_col = head_index // group_size * HD
        query_head = lax.dynamic_slice_in_dim(query_local, head_index * HD, HD, 1)
        grad_head = lax.dynamic_slice_in_dim(grad_local, head_index * HD, HD, 1)
        key_head = lax.dynamic_slice_in_dim(key_flat, kv_col, HD, 1)
        value_head = lax.dynamic_slice_in_dim(value_flat, kv_col, HD, 1)
        scores = (
            lax.dot_general(
                query_head, key_head, (((1,), (1,)), ((), ())), preferred_element_type=jnp.float32
            )
            * softmax_scale
        )
        scores = jnp.where(visible, scores, -1e30)
        row_peak = jnp.max(scores, 1, keepdims=True)
        exponent = jnp.where(visible, jnp.exp(scores - row_peak), 0.0)
        row_total = jnp.sum(exponent, 1, keepdims=True)
        weights = (exponent / row_total).astype(jnp.bfloat16)
        out_head = jnp.dot(weights, value_head, preferred_element_type=jnp.float32).astype(
            jnp.bfloat16
        )
        grad_weights = lax.dot_general(
            grad_head, value_head, (((1,), (1,)), ((), ())), preferred_element_type=jnp.float32
        )
        weights_wide = weights.astype(jnp.float32)
        row_delta = jnp.sum(weights_wide * grad_weights, 1, keepdims=True)
        grad_scores = (weights_wide * (grad_weights - row_delta)).astype(jnp.bfloat16)
        query_grad_head = (
            jnp.dot(grad_scores, key_head, preferred_element_type=jnp.float32) * softmax_scale
        ).astype(jnp.bfloat16)
        key_term = (
            lax.dot_general(
                grad_scores,
                query_head,
                (((0,), (0,)), ((), ())),
                preferred_element_type=jnp.float32,
            )
            * softmax_scale
        )
        value_term = lax.dot_general(
            weights, grad_head, (((0,), (0,)), ((), ())), preferred_element_type=jnp.float32
        )
        attended = lax.dynamic_update_slice_in_dim(attended, out_head, head_index * HD, 1)
        grad_query = lax.dynamic_update_slice_in_dim(
            grad_query, query_grad_head, head_index * HD, 1
        )
        grad_key = lax.dynamic_update_slice_in_dim(
            grad_key, lax.dynamic_slice_in_dim(grad_key, kv_col, HD, 1) + key_term, kv_col, 1
        )
        grad_value = lax.dynamic_update_slice_in_dim(
            grad_value, lax.dynamic_slice_in_dim(grad_value, kv_col, HD, 1) + value_term, kv_col, 1
        )
        head_stats = jnp.stack((row_peak[:, 0], row_total[:, 0], row_delta[:, 0]))
        row_stats = lax.dynamic_update_index_in_dim(row_stats, head_stats, head_index, 1)
        return (attended, grad_query, grad_key, grad_value, row_stats)

    initial = (
        jnp.zeros(query_local.shape, jnp.bfloat16),
        jnp.zeros(query_local.shape, jnp.bfloat16),
        jnp.zeros((window, kv_cols), jnp.float32),
        jnp.zeros((window, kv_cols), jnp.float32),
        jnp.zeros((3, q_heads, tok_rows), jnp.float32),
    )
    attended, grad_query, grad_key, grad_value, row_stats = lax.fori_loop(
        0, q_heads, one_head, initial
    )
    sent_back = jnp.stack((grad_key, grad_value)).reshape(2, blocks, tok_rows, kv_cols)

    def return_one(step_index, moving):
        moving = shifted(moving, "ctx", -1)
        return moving + lax.dynamic_index_in_dim(
            sent_back, distance - step_index, 1, keepdims=False
        )

    owned_sums = lax.fori_loop(1, blocks, return_one, sent_back[:, distance])
    key_sums = owned_sums[0]
    value_sums = owned_sums[1]
    grad_keys_out = key_sums.astype(jnp.bfloat16)
    grad_values_out = value_sums.astype(jnp.bfloat16)
    return (
        lax.all_to_all(attended, "head", split_axis=0, concat_axis=1, tiled=True),
        lax.all_to_all(grad_query, "head", split_axis=0, concat_axis=1, tiled=True),
        lax.all_to_all(grad_keys_out, "head", split_axis=0, concat_axis=1, tiled=True),
        lax.all_to_all(grad_values_out, "head", split_axis=0, concat_axis=1, tiled=True),
    )


def solution(mesh):
    return jax.shard_map(
        per_device,
        mesh=mesh,
        in_specs=(
            P(("ctx", "head"), None),
            P(("ctx", "head"), None),
            P(("ctx", "head"), None),
            P(("ctx", "head"), None),
            P(),
        ),
        out_specs=(
            P(("ctx", "head"), None),
            P(("ctx", "head"), None),
            P(("ctx", "head"), None),
            P(("ctx", "head"), None),
        ),
        check_vma=False,
    )
```

profile of v0, /device:TPU:8, one launch (start us, length us, event | category | flops | bytes accessed | tf_op | source)
XLA Modules:
  0.0 582.7 jit_solution(15004090900700461348)
XLA Ops:
  2.4 3.4 all-to-all-start.1
  7.5 3.8 all-to-all-done.1
  11.3 3.6 all-to-all-start.2
  15.9 4.1 all-to-all-done.2
  20.7 3.6 all-to-all-start.3
  28.3 7.9 %all-to-all-done.3 = bf16[128,2,2048]{2,0,1:T(8,128)(2,1)S(1)} async-done(((bf16[128,2,2048]{2,0,1:T(8,128)(2,1)}), bf16[128,2,2048]{2,0,1:T(8,128)(2,1)S(1)}, u32[]{:S(2)}, u32[]{:S(2)}) %all-to-all-start.3) | async-done | bytes 1048608 | tf_op jit(solution)/shard_map/all_to_all | solution.py:21
  36.2 4.4 all-to-all-start
  40.6 98.2 %while.53 = (s32[]{:T(128)}, bf16[2,256,512]{2,1,0:T(8,128)(2,1)S(1)}, bf16[2,9,256,512]{3,2,0,1:T(8,128)(2,1)}, s32[]{:T(128)}, s32[]{:T(128)}, /*index=5*/s32[]{:T(128)}) while((s32[]{:T(128)}, bf16[2,256,512]{2,1,0:T(8,128)(2,1)S(1)}, bf16[2,9,256,512]{3,2,0,1:T(8,128)(2,1)}, s32[]{:T(128)}, s32[]{:T(128)}, /*index=5*/s32[]{:T(128)}) %tuple.112), condition=%wide.region_1.2_spmd, body=%wide.region_0.0_spmd.sunk | while | flops 5 | bytes 4194459 | solution.py:43
  42.5 9.5 %collective-permute-done = bf16[2,256,512]{2,1,0:T(8,128)(2,1)S(1)} collective-permute-done((bf16[2,256,512]{2,1,0:T(8,128)(2,1)S(1)}, bf16[2,256,512]{2,1,0:T(8,128)(2,1)S(1)}, u32[]{:S(2)}, u32[]{:S(2)}) %collective-permute-start) | collective-permute-done | bytes 524320 | tf_op jit(solution)/shard_map/while/body/eval_jaxpr/ppermute | solution.py:13
  54.8 9.5 %collective-permute-done = bf16[2,256,512]{2,1,0:T(8,128)(2,1)S(1)} collective-permute-done((bf16[2,256,512]{2,1,0:T(8,128)(2,1)S(1)}, bf16[2,256,512]{2,1,0:T(8,128)(2,1)S(1)}, u32[]{:S(2)}, u32[]{:S(2)}) %collective-permute-start) | collective-permute-done | bytes 524320 | tf_op jit(solution)/shard_map/while/body/eval_jaxpr/ppermute | solution.py:13
  67.1 9.5 %collective-permute-done = bf16[2,256,512]{2,1,0:T(8,128)(2,1)S(1)} collective-permute-done((bf16[2,256,512]{2,1,0:T(8,128)(2,1)S(1)}, bf16[2,256,512]{2,1,0:T(8,128)(2,1)S(1)}, u32[]{:S(2)}, u32[]{:S(2)}) %collective-permute-start) | collective-permute-done | bytes 524320 | tf_op jit(solution)/shard_map/while/body/eval_jaxpr/ppermute | solution.py:13
  79.4 9.5 %collective-permute-done = bf16[2,256,512]{2,1,0:T(8,128)(2,1)S(1)} collective-permute-done((bf16[2,256,512]{2,1,0:T(8,128)(2,1)S(1)}, bf16[2,256,512]{2,1,0:T(8,128)(2,1)S(1)}, u32[]{:S(2)}, u32[]{:S(2)}) %collective-permute-start) | collective-permute-done | bytes 524320 | tf_op jit(solution)/shard_map/while/body/eval_jaxpr/ppermute | solution.py:13
  91.6 9.5 %collective-permute-done = bf16[2,256,512]{2,1,0:T(8,128)(2,1)S(1)} collective-permute-done((bf16[2,256,512]{2,1,0:T(8,128)(2,1)S(1)}, bf16[2,256,512]{2,1,0:T(8,128)(2,1)S(1)}, u32[]{:S(2)}, u32[]{:S(2)}) %collective-permute-start) | collective-permute-done | bytes 524320 | tf_op jit(solution)/shard_map/while/body/eval_jaxpr/ppermute | solution.py:13
  103.9 9.5 %collective-permute-done = bf16[2,256,512]{2,1,0:T(8,128)(2,1)S(1)} collective-permute-done((bf16[2,256,512]{2,1,0:T(8,128)(2,1)S(1)}, bf16[2,256,512]{2,1,0:T(8,128)(2,1)S(1)}, u32[]{:S(2)}, u32[]{:S(2)}) %collective-permute-start) | collective-permute-done | bytes 524320 | tf_op jit(solution)/shard_map/while/body/eval_jaxpr/ppermute | solution.py:13
  116.2 9.5 %collective-permute-done = bf16[2,256,512]{2,1,0:T(8,128)(2,1)S(1)} collective-permute-done((bf16[2,256,512]{2,1,0:T(8,128)(2,1)S(1)}, bf16[2,256,512]{2,1,0:T(8,128)(2,1)S(1)}, u32[]{:S(2)}, u32[]{:S(2)}) %collective-permute-start) | collective-permute-done | bytes 524320 | tf_op jit(solution)/shard_map/while/body/eval_jaxpr/ppermute | solution.py:13
  128.4 9.5 %collective-permute-done = bf16[2,256,512]{2,1,0:T(8,128)(2,1)S(1)} collective-permute-done((bf16[2,256,512]{2,1,0:T(8,128)(2,1)S(1)}, bf16[2,256,512]{2,1,0:T(8,128)(2,1)S(1)}, u32[]{:S(2)}, u32[]{:S(2)}) %collective-permute-start) | collective-permute-done | bytes 524320 | tf_op jit(solution)/shard_map/while/body/eval_jaxpr/ppermute | solution.py:13
  138.8 4.3 fusion.41
  149.8 232.5 %while.55 = (s32[]{:T(128)}, bf16[256,2048]{1,0:T(8,128)(2,1)S(1)}, bf16[256,2048]{1,0:T(8,128)(2,1)}, f32[2304,512]{1,0:T(8,128)}, f32[2304,512]{1,0:T(8,128)},...) while((s32[]{:T(128)}, bf16[256,2048]{1,0:T(8,128)(2,1)S(1)}, ...), condition=%wide.region_6.7_spmd.clone, body=%wide.region_2.6_spmd.clone.sunk | while | flops 924056832 | bytes 27604888 | solution.py:120
  155.8 3.0 fusion.77
  170.3 3.0 fusion.77
  184.8 3.0 fusion.77
  199.3 3.0 fusion.77
  213.8 2.9 fusion.77
  216.8 2.9 fusion.78
  228.4 2.9 fusion.77
  231.3 2.9 fusion.78
  242.9 2.9 fusion.77
  245.8 2.9 fusion.78
  257.4 2.9 fusion.77
  260.3 2.9 fusion.78
  274.8 3.0 fusion.78
  289.3 3.0 fusion.78
  303.8 3.0 fusion.78
  318.3 3.0 fusion.78
  329.9 2.9 fusion.77
  332.8 3.0 fusion.78
  344.5 2.9 fusion.77
  347.4 3.0 fusion.78
  359.1 2.9 fusion.77
  362.0 3.0 fusion.78
  373.7 2.9 fusion.77
  376.6 3.0 fusion.78
  382.3 9.1 %pad_maximum_fusion = f32[2,9,256,512]{3,2,0,1:T(8,128)} fusion(f32[1,9,256,512]{3,2,0,1:T(8,128)} %bitcast.78, f32[1,9,256,512]{3,2,0,1:T(8,128)} %bitcast.76), kind=kLoop, calls=%fused_computation.41 | loop fusion | flops 2359296 | bytes 18874368 | tf_op jit(solution)/shard_map/stack | solution.py:123
  391.5 144.9 %while.54 = (s32[]{:T(128)}, f32[2,256,512]{2,1,0:T(8,128)S(1)}, f32[2,9,256,512]{3,2,0,1:T(8,128)}, s32[]{:T(128)}, s32[]{:T(128)}, /*index=5*/s32[]{:T(128)}, s32[]{:T(128)}) while((s32[]{:T(128)}, f32[2,256,512]{2,1,0:T(8,128)S(1)}, f32[2,9,256,512]{3,2,0,1:T(8,128)}, s32[]{:T(128)}, s32[]{:T(128)}, /*index=5*/s32[]{:T(128)}, ...), condition=%wide.region_8.9_spmd, body=%wide.region_7.8_spmd.sunk | while | flops 262150 | bytes 7340199 | solution.py:131
  393.4 12.3 %collective-permute-done.1 = f32[2,256,512]{2,1,0:T(8,128)S(1)} collective-permute-done((f32[2,256,512]{2,1,0:T(8,128)S(1)}, f32[2,256,512]{2,1,0:T(8,128)S(1)}, u32[]{:S(2)}, u32[]{:S(2)}) %collective-permute-start.1) | collective-permute-done | bytes 1048608 | tf_op jit(solution)/shard_map/while/body/eval_jaxpr/ppermute | solution.py:13
  407.1 4.7 collective-permute-start.1
  411.9 12.3 %collective-permute-done.1 = f32[2,256,512]{2,1,0:T(8,128)S(1)} collective-permute-done((f32[2,256,512]{2,1,0:T(8,128)S(1)}, f32[2,256,512]{2,1,0:T(8,128)S(1)}, u32[]{:S(2)}, u32[]{:S(2)}) %collective-permute-start.1) | collective-permute-done | bytes 1048608 | tf_op jit(solution)/shard_map/while/body/eval_jaxpr/ppermute | solution.py:13
  425.6 4.7 collective-permute-start.1
  430.3 12.3 %collective-permute-done.1 = f32[2,256,512]{2,1,0:T(8,128)S(1)} collective-permute-done((f32[2,256,512]{2,1,0:T(8,128)S(1)}, f32[2,256,512]{2,1,0:T(8,128)S(1)}, u32[]{:S(2)}, u32[]{:S(2)}) %collective-permute-start.1) | collective-permute-done | bytes 1048608 | tf_op jit(solution)/shard_map/while/body/eval_jaxpr/ppermute | solution.py:13
  444.1 4.7 collective-permute-start.1
  448.8 12.3 %collective-permute-done.1 = f32[2,256,512]{2,1,0:T(8,128)S(1)} collective-permute-done((f32[2,256,512]{2,1,0:T(8,128)S(1)}, f32[2,256,512]{2,1,0:T(8,128)S(1)}, u32[]{:S(2)}, u32[]{:S(2)}) %collective-permute-start.1) | collective-permute-done | bytes 1048608 | tf_op jit(solution)/shard_map/while/body/eval_jaxpr/ppermute | solution.py:13
  462.5 4.7 collective-permute-start.1
  467.3 12.3 %collective-permute-done.1 = f32[2,256,512]{2,1,0:T(8,128)S(1)} collective-permute-done((f32[2,256,512]{2,1,0:T(8,128)S(1)}, f32[2,256,512]{2,1,0:T(8,128)S(1)}, u32[]{:S(2)}, u32[]{:S(2)}) %collective-permute-start.1) | collective-permute-done | bytes 1048608 | tf_op jit(solution)/shard_map/while/body/eval_jaxpr/ppermute | solution.py:13
  481.0 4.7 collective-permute-start.1
  485.7 12.3 %collective-permute-done.1 = f32[2,256,512]{2,1,0:T(8,128)S(1)} collective-permute-done((f32[2,256,512]{2,1,0:T(8,128)S(1)}, f32[2,256,512]{2,1,0:T(8,128)S(1)}, u32[]{:S(2)}, u32[]{:S(2)}) %collective-permute-start.1) | collective-permute-done | bytes 1048608 | tf_op jit(solution)/shard_map/while/body/eval_jaxpr/ppermute | solution.py:13
  499.5 4.7 collective-permute-start.1
  504.2 12.3 %collective-permute-done.1 = f32[2,256,512]{2,1,0:T(8,128)S(1)} collective-permute-done((f32[2,256,512]{2,1,0:T(8,128)S(1)}, f32[2,256,512]{2,1,0:T(8,128)S(1)}, u32[]{:S(2)}, u32[]{:S(2)}) %collective-permute-start.1) | collective-permute-done | bytes 1048608 | tf_op jit(solution)/shard_map/while/body/eval_jaxpr/ppermute | solution.py:13
  517.9 4.7 collective-permute-start.1
  522.7 12.3 %collective-permute-done.1 = f32[2,256,512]{2,1,0:T(8,128)S(1)} collective-permute-done((f32[2,256,512]{2,1,0:T(8,128)S(1)}, f32[2,256,512]{2,1,0:T(8,128)S(1)}, u32[]{:S(2)}, u32[]{:S(2)}) %collective-permute-start.1) | collective-permute-done | bytes 1048608 | tf_op jit(solution)/shard_map/while/body/eval_jaxpr/ppermute | solution.py:13
  536.5 9.3 %all_to_all.140 = bf16[2,128,512]{2,1,0:T(8,128)(2,1)} all-to-all(bf16[2,128,512]{2,1,0:T(8,128)(2,1)S(1)} %bitcast.94), channel_id=1, replica_groups=mesh['ctx'=16,'head'=2] {'head'}, dimensions={0} | all-to-all | bytes 524288 | tf_op jit(solution)/shard_map/all_to_all | solution.py:139
  545.8 7.6 %all_to_all.141 = bf16[2,128,512]{2,1,0:T(8,128)(2,1)S(1)} all-to-all(bf16[2,128,512]{2,1,0:T(8,128)(2,1)S(1)} %bitcast.93), channel_id=1, replica_groups=mesh['ctx'=16,'head'=2] {'head'}, dimensions={0} | all-to-all | bytes 524288 | tf_op jit(solution)/shard_map/all_to_all | solution.py:140
  553.3 14.4 %all_to_all.142 = bf16[2,128,2048]{2,1,0:T(8,128)(2,1)S(1)} all-to-all(bf16[2,128,2048]{2,1,0:T(8,128)(2,1)S(1)} %bitcast.82), channel_id=1, replica_groups=mesh['ctx'=16,'head'=2] {'head'}, dimensions={0} | all-to-all | bytes 2097152 | tf_op jit(solution)/shard_map/all_to_all | solution.py:137
  567.8 3.6 all-to-all-start.5
  576.3 4.4 all-to-all-done.5
  (182 shorter events, 219.5 us)
Async XLA Ops:
  0.6 14.2 %copy-start.3 = (bf16[128,4096]{1,0:T(8,128)(2,1)S(1)}, bf16[128,4096]{1,0:T(8,128)(2,1)}, u32[]{:S(2)}) copy-start(bf16[128,4096]{1,0:T(8,128)(2,1)} %param.16) | copy-start | bytes 3145732
  2.4 8.9 %all-to-all-start.1 = ((bf16[128,2,512]{2,0,1:T(8,128)(2,1)}), bf16[128,2,512]{2,0,1:T(8,128)(2,1)S(1)}, u32[]{:S(2)}, u32[]{:S(2)}) async-start(bf16[128,2,512]{2,0,1:T(8,128)(2,1)} %bitcast.63), calls=%async_computation.1 | async-start | bytes 524288 | tf_op jit(solution)/shard_map/all_to_all | solution.py:19
  11.3 13.1 %copy-start.7 = (s32[4096]{0:T(1024)S(1)}, s32[4096]{0:T(1024)}, u32[]{:S(2)}) copy-start(s32[4096]{0:T(1024)} %param.17) | copy-start | bytes 49156
  11.3 13.3 %copy-start.4 = (bf16[128,4096]{1,0:T(8,128)(2,1)S(1)}, bf16[128,4096]{1,0:T(8,128)(2,1)}, u32[]{:S(2)}) copy-start(bf16[128,4096]{1,0:T(8,128)(2,1)} %param.13) | copy-start | bytes 3145732
  11.3 8.7 %all-to-all-start.2 = ((bf16[128,2,512]{2,0,1:T(8,128)(2,1)}), bf16[128,2,512]{2,0,1:T(8,128)(2,1)S(1)}, u32[]{:S(2)}, u32[]{:S(2)}) async-start(bf16[128,2,512]{2,0,1:T(8,128)(2,1)} %bitcast.62), calls=%async_computation.2 | async-start | bytes 524288 | tf_op jit(solution)/shard_map/all_to_all | solution.py:20
  20.0 0.7 copy-start.5
  20.7 15.4 %all-to-all-start.3 = ((bf16[128,2,2048]{2,0,1:T(8,128)(2,1)}), bf16[128,2,2048]{2,0,1:T(8,128)(2,1)S(1)}, u32[]{:S(2)}, u32[]{:S(2)}) async-start(bf16[128,2,2048]{2,0,1:T(8,128)(2,1)} %bitcast.60), calls=%async_computation.3 | async-start | bytes 2097152 | tf_op jit(solution)/shard_map/all_to_all | solution.py:21
  24.3 1.3 copy-start.6
  36.2 4.4 copy-start.2
  36.2 106.8 %all-to-all-start = ((bf16[128,2,2048]{2,0,1:T(8,128)(2,1)}), bf16[128,2,2048]{2,0,1:T(8,128)(2,1)}, u32[]{:S(2)}, u32[]{:S(2)}) async-start(bf16[128,2,2048]{2,0,1:T(8,128)(2,1)} %bitcast.61), calls=%async_computation | async-start | bytes 2097152 | tf_op jit(solution)/shard_map/all_to_all | solution.py:18
  40.6 11.4 %collective-permute-start = (bf16[2,256,512]{2,1,0:T(8,128)(2,1)S(1)}, bf16[2,256,512]{2,1,0:T(8,128)(2,1)S(1)}, u32[]{:S(2)}, u32[]{:S(2)}) collective-permute-start(bf16[2,256,512]{2,1,0:T(8,128)(2,1)S(1)} %get-tuple-element.639), channel_id=1, source_target_pairs={{0,2},{2,4},{4,6},{6,8},{8,10},{10,12},{12,14},{14,16},{16,18},{18... | collective-permute-start | bytes 1572872 | tf_op jit(solution)/shard_map/while/body/eval_jaxpr/ppermute | solution.py:13
  52.9 11.4 %collective-permute-start = (bf16[2,256,512]{2,1,0:T(8,128)(2,1)S(1)}, bf16[2,256,512]{2,1,0:T(8,128)(2,1)S(1)}, u32[]{:S(2)}, u32[]{:S(2)}) collective-permute-start(bf16[2,256,512]{2,1,0:T(8,128)(2,1)S(1)} %get-tuple-element.639), channel_id=1, source_target_pairs={{0,2},{2,4},{4,6},{6,8},{8,10},{10,12},{12,14},{14,16},{16,18},{18... | collective-permute-start | bytes 1572872 | tf_op jit(solution)/shard_map/while/body/eval_jaxpr/ppermute | solution.py:13
  65.2 11.4 %collective-permute-start = (bf16[2,256,512]{2,1,0:T(8,128)(2,1)S(1)}, bf16[2,256,512]{2,1,0:T(8,128)(2,1)S(1)}, u32[]{:S(2)}, u32[]{:S(2)}) collective-permute-start(bf16[2,256,512]{2,1,0:T(8,128)(2,1)S(1)} %get-tuple-element.639), channel_id=1, source_target_pairs={{0,2},{2,4},{4,6},{6,8},{8,10},{10,12},{12,14},{14,16},{16,18},{18... | collective-permute-start | bytes 1572872 | tf_op jit(solution)/shard_map/while/body/eval_jaxpr/ppermute | solution.py:13
  77.4 11.4 %collective-permute-start = (bf16[2,256,512]{2,1,0:T(8,128)(2,1)S(1)}, bf16[2,256,512]{2,1,0:T(8,128)(2,1)S(1)}, u32[]{:S(2)}, u32[]{:S(2)}) collective-permute-start(bf16[2,256,512]{2,1,0:T(8,128)(2,1)S(1)} %get-tuple-element.639), channel_id=1, source_target_pairs={{0,2},{2,4},{4,6},{6,8},{8,10},{10,12},{12,14},{14,16},{16,18},{18... | collective-permute-start | bytes 1572872 | tf_op jit(solution)/shard_map/while/body/eval_jaxpr/ppermute | solution.py:13
  89.7 11.4 %collective-permute-start = (bf16[2,256,512]{2,1,0:T(8,128)(2,1)S(1)}, bf16[2,256,512]{2,1,0:T(8,128)(2,1)S(1)}, u32[]{:S(2)}, u32[]{:S(2)}) collective-permute-start(bf16[2,256,512]{2,1,0:T(8,128)(2,1)S(1)} %get-tuple-element.639), channel_id=1, source_target_pairs={{0,2},{2,4},{4,6},{6,8},{8,10},{10,12},{12,14},{14,16},{16,18},{18... | collective-permute-start | bytes 1572872 | tf_op jit(solution)/shard_map/while/body/eval_jaxpr/ppermute | solution.py:13
  102.0 11.4 %collective-permute-start = (bf16[2,256,512]{2,1,0:T(8,128)(2,1)S(1)}, bf16[2,256,512]{2,1,0:T(8,128)(2,1)S(1)}, u32[]{:S(2)}, u32[]{:S(2)}) collective-permute-start(bf16[2,256,512]{2,1,0:T(8,128)(2,1)S(1)} %get-tuple-element.639), channel_id=1, source_target_pairs={{0,2},{2,4},{4,6},{6,8},{8,10},{10,12},{12,14},{14,16},{16,18},{18... | collective-permute-start | bytes 1572872 | tf_op jit(solution)/shard_map/while/body/eval_jaxpr/ppermute | solution.py:13
  114.2 11.4 %collective-permute-start = (bf16[2,256,512]{2,1,0:T(8,128)(2,1)S(1)}, bf16[2,256,512]{2,1,0:T(8,128)(2,1)S(1)}, u32[]{:S(2)}, u32[]{:S(2)}) collective-permute-start(bf16[2,256,512]{2,1,0:T(8,128)(2,1)S(1)} %get-tuple-element.639), channel_id=1, source_target_pairs={{0,2},{2,4},{4,6},{6,8},{8,10},{10,12},{12,14},{14,16},{16,18},{18... | collective-permute-start | bytes 1572872 | tf_op jit(solution)/shard_map/while/body/eval_jaxpr/ppermute | solution.py:13
  126.5 11.4 %collective-permute-start = (bf16[2,256,512]{2,1,0:T(8,128)(2,1)S(1)}, bf16[2,256,512]{2,1,0:T(8,128)(2,1)S(1)}, u32[]{:S(2)}, u32[]{:S(2)}) collective-permute-start(bf16[2,256,512]{2,1,0:T(8,128)(2,1)S(1)} %get-tuple-element.639), channel_id=1, source_target_pairs={{0,2},{2,4},{4,6},{6,8},{8,10},{10,12},{12,14},{14,16},{16,18},{18... | collective-permute-start | bytes 1572872 | tf_op jit(solution)/shard_map/while/body/eval_jaxpr/ppermute | solution.py:13
  382.3 9.1 %copy-start = (f32[2304,512]{1,0:T(8,128)S(1)}, f32[2304,512]{1,0:T(8,128)}, u32[]{:S(2)}) copy-start(f32[2304,512]{1,0:T(8,128)} %get-tuple-element.417) | copy-start | bytes 14155780
  382.3 9.1 %copy-start.1 = (f32[2304,512]{1,0:T(8,128)S(1)}, f32[2304,512]{1,0:T(8,128)}, u32[]{:S(2)}) copy-start(f32[2304,512]{1,0:T(8,128)} %get-tuple-element.418) | copy-start | bytes 14155780
  391.5 14.2 %collective-permute-start.1 = (f32[2,256,512]{2,1,0:T(8,128)S(1)}, f32[2,256,512]{2,1,0:T(8,128)S(1)}, u32[]{:S(2)}, u32[]{:S(2)}) collective-permute-start(f32[2,256,512]{2,1,0:T(8,128)S(1)} %get-tuple-element.721), channel_id=1, source_target_pairs={{2,0},{4,2},{6,4},{8,6},{10,8},{12,10},{14,12},{16,14},{18,16},{20... | collective-permute-start | bytes 3145736 | tf_op jit(solution)/shard_map/while/body/eval_jaxpr/ppermute | solution.py:13
  407.1 17.0 %collective-permute-start.1 = (f32[2,256,512]{2,1,0:T(8,128)S(1)}, f32[2,256,512]{2,1,0:T(8,128)S(1)}, u32[]{:S(2)}, u32[]{:S(2)}) collective-permute-start(f32[2,256,512]{2,1,0:T(8,128)S(1)} %get-tuple-element.721), channel_id=1, source_target_pairs={{2,0},{4,2},{6,4},{8,6},{10,8},{12,10},{14,12},{16,14},{18,16},{20... | collective-permute-start | bytes 3145736 | tf_op jit(solution)/shard_map/while/body/eval_jaxpr/ppermute | solution.py:13
  425.6 17.0 %collective-permute-start.1 = (f32[2,256,512]{2,1,0:T(8,128)S(1)}, f32[2,256,512]{2,1,0:T(8,128)S(1)}, u32[]{:S(2)}, u32[]{:S(2)}) collective-permute-start(f32[2,256,512]{2,1,0:T(8,128)S(1)} %get-tuple-element.721), channel_id=1, source_target_pairs={{2,0},{4,2},{6,4},{8,6},{10,8},{12,10},{14,12},{16,14},{18,16},{20... | collective-permute-start | bytes 3145736 | tf_op jit(solution)/shard_map/while/body/eval_jaxpr/ppermute | solution.py:13
  444.1 17.0 %collective-permute-start.1 = (f32[2,256,512]{2,1,0:T(8,128)S(1)}, f32[2,256,512]{2,1,0:T(8,128)S(1)}, u32[]{:S(2)}, u32[]{:S(2)}) collective-permute-start(f32[2,256,512]{2,1,0:T(8,128)S(1)} %get-tuple-element.721), channel_id=1, source_target_pairs={{2,0},{4,2},{6,4},{8,6},{10,8},{12,10},{14,12},{16,14},{18,16},{20... | collective-permute-start | bytes 3145736 | tf_op jit(solution)/shard_map/while/body/eval_jaxpr/ppermute | solution.py:13
  462.5 17.0 %collective-permute-start.1 = (f32[2,256,512]{2,1,0:T(8,128)S(1)}, f32[2,256,512]{2,1,0:T(8,128)S(1)}, u32[]{:S(2)}, u32[]{:S(2)}) collective-permute-start(f32[2,256,512]{2,1,0:T(8,128)S(1)} %get-tuple-element.721), channel_id=1, source_target_pairs={{2,0},{4,2},{6,4},{8,6},{10,8},{12,10},{14,12},{16,14},{18,16},{20... | collective-permute-start | bytes 3145736 | tf_op jit(solution)/shard_map/while/body/eval_jaxpr/ppermute | solution.py:13
  481.0 17.0 %collective-permute-start.1 = (f32[2,256,512]{2,1,0:T(8,128)S(1)}, f32[2,256,512]{2,1,0:T(8,128)S(1)}, u32[]{:S(2)}, u32[]{:S(2)}) collective-permute-start(f32[2,256,512]{2,1,0:T(8,128)S(1)} %get-tuple-element.721), channel_id=1, source_target_pairs={{2,0},{4,2},{6,4},{8,6},{10,8},{12,10},{14,12},{16,14},{18,16},{20... | collective-permute-start | bytes 3145736 | tf_op jit(solution)/shard_map/while/body/eval_jaxpr/ppermute | solution.py:13
  499.5 17.0 %collective-permute-start.1 = (f32[2,256,512]{2,1,0:T(8,128)S(1)}, f32[2,256,512]{2,1,0:T(8,128)S(1)}, u32[]{:S(2)}, u32[]{:S(2)}) collective-permute-start(f32[2,256,512]{2,1,0:T(8,128)S(1)} %get-tuple-element.721), channel_id=1, source_target_pairs={{2,0},{4,2},{6,4},{8,6},{10,8},{12,10},{14,12},{16,14},{18,16},{20... | collective-permute-start | bytes 3145736 | tf_op jit(solution)/shard_map/while/body/eval_jaxpr/ppermute | solution.py:13
  517.9 17.0 %collective-permute-start.1 = (f32[2,256,512]{2,1,0:T(8,128)S(1)}, f32[2,256,512]{2,1,0:T(8,128)S(1)}, u32[]{:S(2)}, u32[]{:S(2)}) collective-permute-start(f32[2,256,512]{2,1,0:T(8,128)S(1)} %get-tuple-element.721), channel_id=1, source_target_pairs={{2,0},{4,2},{6,4},{8,6},{10,8},{12,10},{14,12},{16,14},{18,16},{20... | collective-permute-start | bytes 3145736 | tf_op jit(solution)/shard_map/while/body/eval_jaxpr/ppermute | solution.py:13
  567.8 13.0 %all-to-all-start.5 = ((bf16[2,128,2048]{2,1,0:T(8,128)(2,1)}), bf16[2,128,2048]{2,1,0:T(8,128)(2,1)S(1)}, u32[]{:S(2)}, u32[]{:S(2)}) async-start(bf16[2,128,2048]{2,1,0:T(8,128)(2,1)} %bitcast.83), calls=%async_computation.5 | async-start | bytes 2097152 | tf_op jit(solution)/shard_map/all_to_all | solution.py:138
where the time goes:
time: 587 us; the launch traced here: 583 us
  matrix products  209 us (36%)
  waiting for transfers between devices  194 us (33%)
  starting transfers between devices  68.8 us (12%)
  other arithmetic  43.9 us (7%)
  local copies, waits for them, and re-layouts  34 us (6%)
  blocking collectives  31.3 us (5%)
    ppermute x16, waiting for transfers between devices, shifted(): return lax.ppermute(value, axis, pairs)  174 us
    ppermute x16, starting transfers between devices, shifted(): return lax.ppermute(value, axis, pairs)  50.2 us
    dot_general x16, matrix products, one_head(): lax.dot_general(weights, grad_head, (((0,), (0,)), ((), ())), preferred_e...  47.2 us
    dot_general x16, matrix products, one_head(): lax.dot_general(grad_scores, query_head, (((0,), (0,)), ((), ())), prefer...  46.9 us
    dot_general x16, matrix products, one_head(): lax.dot_general(grad_head, value_head, (((1,), (1,)), ((), ())), preferre...  37.1 us
    dot_general x16, matrix products, one_head(): lax.dot_general(query_head, key_head, (((1,), (1,)), ((), ())), preferred...  34.9 us
    dot_general x16, matrix products, one_head(): jnp.dot(grad_scores, key_head, preferred_element_type=jnp.float32)  34.7 us
    reduce_sum x16, other arithmetic, one_head(): row_total = jnp.sum(exponent, 1, keepdims=True)  17.4 us
  transfers between devices with their start and end apart: 21, of which 20 were waited for; matrix products, arithmetic and copies ran while one was open for 4% of the time, Pallas kernels for 0%

commit v1 on v0

v1 whole, which is shorter than its diff:
```python
import functools

import jax
import jax.numpy as jnp
from jax import lax
from jax.experimental import pallas as pl
from jax.experimental.pallas import tpu as pltpu
from jax.sharding import PartitionSpec as P

HD = 128
DOC_MOST = 2048
TILE = 256
LOG2E = 1.4426950408889634
MESH = pl.DeviceIdType.MESH


def place(ctx_low, heads):
    ctx, head = lax.axis_index("ctx"), lax.axis_index("head")
    block = ctx // ctx_low
    me = (ctx - block * ctx_low) * heads + head

    def member(number):
        return (block * ctx_low + number // heads, lax.rem(number, heads))

    return ctx, head, block, me, member


def greet(members, ctx, head, ctx_low, has_prev, has_next):
    barrier = pltpu.get_barrier_semaphore()
    for device in members:
        pl.semaphore_signal(barrier, inc=1, device_id=device, device_id_type=MESH)

    @pl.when(has_prev)
    def _():
        pl.semaphore_signal(barrier, inc=1, device_id=(ctx - ctx_low, head), device_id_type=MESH)

    @pl.when(has_next)
    def _():
        pl.semaphore_signal(barrier, inc=1, device_id=(ctx + ctx_low, head), device_id_type=MESH)

    near = has_prev.astype(jnp.int32) + has_next.astype(jnp.int32)
    pl.semaphore_wait(barrier, len(members) + near)


def gather_kernel(
    heads, ctx_low, blocks, distance, q_ref, k_ref, v_ref, g_ref,
    qo_ref, go_ref, band_ref, own_sem, send_sem, recv_sem, hop_send, hop_recv,
):
    group = ctx_low * heads
    rows = q_ref.shape[0]
    q_cols = q_ref.shape[1] // group
    ctx, head, block, me, member = place(ctx_low, heads)
    has_prev, has_next = block > 0, block < blocks - 1
    others = [lax.rem(me + step, group) for step in range(1, group)]
    greet([member(o) for o in others], ctx, head, ctx_low, has_prev, has_next)
    mine = pl.ds(pl.multiple_of(me * rows, rows), rows)
    parts = (
        (k_ref, HD, band_ref.at[distance, 0]),
        (v_ref, HD, band_ref.at[distance, 1]),
        (q_ref, q_cols, qo_ref),
        (g_ref, q_cols, go_ref),
    )

    def piece(ref, width, number):
        return ref.at[:, pl.ds(pl.multiple_of(number * width, width), width)]

    own, copies = [], []
    for a, (src, width, dst) in enumerate(parts):
        local = pltpu.make_async_copy(piece(src, width, me), dst.at[mine], own_sem.at[a])
        local.start()
        own.append(local)
        line = []
        for step, other in enumerate(others):
            copy = pltpu.make_async_remote_copy(
                src_ref=piece(src, width, other), dst_ref=dst.at[mine],
                send_sem=send_sem.at[a, step], recv_sem=recv_sem.at[a, step],
                device_id=member(other), device_id_type=MESH,
            )
            copy.start()
            line.append(copy)
        copies.append(line)

    def hop(step, c):
        return pltpu.make_async_remote_copy(
            src_ref=band_ref.at[distance - step, c], dst_ref=band_ref.at[distance - step - 1, c],
            send_sem=hop_send.at[step, c], recv_sem=hop_recv.at[step, c],
            device_id=(ctx + ctx_low, head), device_id_type=MESH,
        )

    for step in range(distance):
        for c in range(2):
            if step == 0:
                own[c].wait()
                for copy in copies[c]:
                    copy.wait_recv()
            else:
                @pl.when(block - step >= 0)
                def _():
                    hop(step - 1, c).wait_recv()

            @pl.when((block - step >= 0) & has_next)
            def _():
                hop(step, c).start()

    for a in range(2, 4):
        own[a].wait()
        for copy in copies[a]:
            copy.wait_recv()
    for line in copies:
        for copy in line:
            copy.wait_send()
    for c in range(2):
        @pl.when(block - distance >= 0)
        def _():
            hop(distance - 1, c).wait_recv()

        for step in range(distance):
            @pl.when((block - step >= 0) & has_next)
            def _():
                hop(step, c).wait_send()


def return_kernel(
    heads, ctx_low, blocks, distance, a_ref, d_ref, part_ref,
    ao_ref, do_ref, ko_ref, vo_ref, sums, landed, own_sem, send_sem, recv_sem, hop_send, hop_recv,
):
    group = ctx_low * heads
    rows = ao_ref.shape[0]
    q_cols = a_ref.shape[1]
    ctx, head, block, me, member = place(ctx_low, heads)
    has_prev, has_next = block > 0, block < blocks - 1
    others = [lax.rem(me + step, group) for step in range(1, group)]
    greet([member(o) for o in others], ctx, head, ctx_low, has_prev, has_next)

    def hop(step, c):
        source = part_ref.at[0, c] if step == 0 else sums.at[step - 1, c]
        return pltpu.make_async_remote_copy(
            src_ref=source, dst_ref=landed.at[step, c],
            send_sem=hop_send.at[step, c], recv_sem=hop_recv.at[step, c],
            device_id=(ctx - ctx_low, head), device_id_type=MESH,
        )

    def pieces(number):
        return pl.ds(pl.multiple_of(number * rows, rows), rows)

    own, copies = [], []

    def send(a, src, width, dst):
        column = pl.ds(pl.multiple_of(me * width, width), width)
        local = pltpu.make_async_copy(src.at[pieces(me)], dst.at[:, column], own_sem.at[a])
        local.start()
        own.append(local)
        for step, other in enumerate(others):
            copy = pltpu.make_async_remote_copy(
                src_ref=src.at[pieces(other)], dst_ref=dst.at[:, column],
                send_sem=send_sem.at[a, step], recv_sem=recv_sem.at[a, step],
                device_id=member(other), device_id_type=MESH,
            )
            copy.start()
            copies.append(copy)

    for c in range(2):
        @pl.when(block - distance >= 0)
        def _():
            hop(0, c).start()

    send(0, a_ref, q_cols, ao_ref)
    send(1, d_ref, q_cols, do_ref)

    for step in range(1, distance + 1):
        valid = block - (distance - step) >= 0
        for c in range(2):
            @pl.when(valid & has_next)
            def _():
                hop(step - 1, c).wait_recv()
                both = part_ref[step, c].astype(jnp.float32) + landed[step - 1, c].astype(jnp.float32)
                sums[step - 1, c] = both.astype(jnp.bfloat16)

            @pl.when(valid & jnp.logical_not(has_next))
            def _():
                sums[step - 1, c] = part_ref[step, c]

            if step < distance:
                @pl.when(valid)
                def _():
                    hop(step, c).start()

    send(2, sums.at[distance - 1, 0], HD, ko_ref)
    send(3, sums.at[distance - 1, 1], HD, vo_ref)
    for local in own:
        local.wait()
    for copy in copies:
        copy.wait()
    for c in range(2):
        for step in range(distance):
            @pl.when(block - (distance - step) >= 0)
            def _():
                hop(step, c).wait_send()


def attend_kernel(
    distance, scale, sc_ref, start_ref, q_ref, g_ref, band_ref, att_ref, dq_ref, part_ref,
    acc, kept, qc, qt, gc, gt, peak, total, ot, dqt, kt, vt,
):
    tokens = q_ref.shape[0]
    share = q_ref.shape[1] // HD
    factor = scale * LOG2E
    per_block = tokens // TILE
    base = sc_ref[0]
    first_token = base - distance * tokens
    tiles = tokens // TILE

    acc[...] = jnp.zeros_like(acc)

    def turn(slot, _):
        for t in range(per_block):
            kt[slot * per_block + t] = band_ref[slot, 0, t * TILE:(t + 1) * TILE, :].T
            vt[slot * per_block + t] = band_ref[slot, 1, t * TILE:(t + 1) * TILE, :].T
        return 0

    lax.fori_loop(0, distance + 1, turn, 0)

    def key_tile(kb, c):
        slot = kb // per_block
        offset = pl.multiple_of((kb - slot * per_block) * TILE, TILE)
        return band_ref[slot, c, pl.ds(offset, TILE), :]

    def fold(x, op):
        return op(x.reshape(TILE // 8, 8, TILE), 0)

    def one_tile(i, _):
        row = pl.multiple_of(i * TILE, TILE)
        here = pl.ds(row, TILE)
        low, high = sc_ref[1 + 2 * i], sc_ref[2 + 2 * i]
        kb0 = (low - first_token) // TILE
        kb1 = distance * per_block + i
        for h in range(share):
            span = slice(h * TILE, (h + 1) * TILE)
            head = slice(h * HD, (h + 1) * HD)
            qc[span, :] = q_ref[here, head]
            gc[span, :] = g_ref[here, head]
            qt[:, span] = q_ref[here, head].T
            gt[:, span] = g_ref[here, head].T
        peak[...] = jnp.full_like(peak, -1e30)
        total[...] = jnp.zeros_like(total)
        ot[...] = jnp.zeros_like(ot)
        dqt[...] = jnp.zeros_like(dqt)
        starts = start_ref[:, here]

        def score(kb, _):
            keys = key_tile(kb, 0)
            tile_token = first_token + kb * TILE
            masked = (kb == kb1) | (high > tile_token)

            @pl.when(masked)
            def _():
                col = tile_token + lax.broadcasted_iota(jnp.int32, (TILE, TILE), 0)
                token = base + row + lax.broadcasted_iota(jnp.int32, (TILE, TILE), 1)
                seen = (col >= starts) & (col <= token)
                for h in range(share):
                    span = slice(h * TILE, (h + 1) * TILE)
                    s = jnp.dot(keys, qt[:, span], preferred_element_type=jnp.float32)
                    s = jnp.where(seen, s, -1e30)
                    kept[kb - kb0, :, span] = s
                    peak[:, span] = jnp.maximum(peak[:, span], fold(s, jnp.max))

            @pl.when(jnp.logical_not(masked))
            def _():
                for h in range(share):
                    span = slice(h * TILE, (h + 1) * TILE)
                    s = jnp.dot(keys, qt[:, span], preferred_element_type=jnp.float32)
                    kept[kb - kb0, :, span] = s
                    peak[:, span] = jnp.maximum(peak[:, span], fold(s, jnp.max))

            return 0

        lax.fori_loop(kb0, kb1 + 1, score, 0)
        top = jnp.max(peak[...], 0, keepdims=True) * factor

        def forward(kb, _):
            values_t = vt[kb]
            for h in range(share):
                span = slice(h * TILE, (h + 1) * TILE)
                p = jnp.exp2(kept[kb - kb0, :, span] * factor - top[:, span])
                kept[kb - kb0, :, span] = p
                total[:, span] += fold(p, jnp.sum)
                ot[:, span] += jnp.dot(
                    values_t, p.astype(jnp.bfloat16), preferred_element_type=jnp.float32
                )
            return 0

        lax.fori_loop(kb0, kb1 + 1, forward, 0)
        inverse = 1.0 / jnp.sum(total[...], 0, keepdims=True)
        out = ot[...] * inverse
        delta = jnp.sum(out * gt[...].astype(jnp.float32), 0, keepdims=True)
        for h in range(share):
            span = slice(h * TILE, (h + 1) * TILE)
            att_ref[here, h * HD:(h + 1) * HD] = out[:, span].T.astype(jnp.bfloat16)

        def backward(kb, _):
            values = key_tile(kb, 1)
            keys_t = kt[kb]
            dv = jnp.zeros((TILE, HD), jnp.float32)
            dk = jnp.zeros((TILE, HD), jnp.float32)
            for h in range(share):
                span = slice(h * TILE, (h + 1) * TILE)
                w = kept[kb - kb0, :, span] * inverse[:, span]
                dp = jnp.dot(values, gt[:, span], preferred_element_type=jnp.float32)
                ds = (w * (dp - delta[:, span])).astype(jnp.bfloat16)
                dv += jnp.dot(
                    w.astype(jnp.bfloat16), gc[span, :], preferred_element_type=jnp.float32
                )
                dk += jnp.dot(ds, qc[span, :], preferred_element_type=jnp.float32)
                dqt[:, span] += jnp.dot(keys_t, ds, preferred_element_type=jnp.float32)
            where = pl.ds(pl.multiple_of(kb * TILE, TILE), TILE)
            acc[0, where, :] += dk
            acc[1, where, :] += dv
            return 0

        lax.fori_loop(kb0, kb1 + 1, backward, 0)
        for h in range(share):
            span = slice(h * TILE, (h + 1) * TILE)
            dq_ref[here, h * HD:(h + 1) * HD] = (dqt[:, span] * scale).T.astype(jnp.bfloat16)
        return 0

    lax.fori_loop(0, tiles, one_tile, 0)
    for slot in range(distance + 1):
        span = slice(slot * tokens, (slot + 1) * tokens)
        part_ref[slot, 0] = (acc[0, span, :] * scale).astype(jnp.bfloat16)
        part_ref[slot, 1] = acc[1, span, :].astype(jnp.bfloat16)


def per_device(queries, keys, values, grad_out, doc_ids):
    heads = lax.axis_size("head")
    peers = lax.axis_size("ctx")
    rows = queries.shape[0]
    kv_heads = keys.shape[1] // HD
    q_heads = queries.shape[1] // HD
    share = q_heads // kv_heads
    ctx_low = kv_heads // heads
    blocks = peers // ctx_low
    tokens = rows * kv_heads
    distance = DOC_MOST // tokens
    group = kv_heads
    bf16, f32 = jnp.bfloat16, jnp.float32
    vmem = pl.BlockSpec(memory_space=pltpu.VMEM)
    smem = pl.BlockSpec(memory_space=pltpu.SMEM)
    dma = pltpu.SemaphoreType.DMA
    limit = 60 * 1024 * 1024

    q_all, g_all, band = pl.pallas_call(
        functools.partial(gather_kernel, heads, ctx_low, blocks, distance),
        out_shape=(
            jax.ShapeDtypeStruct((tokens, share * HD), bf16),
            jax.ShapeDtypeStruct((tokens, share * HD), bf16),
            jax.ShapeDtypeStruct((distance + 1, 2, tokens, HD), bf16),
        ),
        in_specs=[vmem] * 4,
        out_specs=(vmem,) * 3,
        scratch_shapes=[
            dma((4,)), dma((4, group - 1)), dma((4, group - 1)),
            dma((distance, 2)), dma((distance, 2)),
        ],
        compiler_params=pltpu.CompilerParams(
            collective_id=1, has_side_effects=True, vmem_limit_bytes=limit
        ),
        name="gather",
    )(queries, keys, values, grad_out)

    block = lax.axis_index("ctx") // ctx_low
    base = block * tokens
    padded = jnp.concatenate((jnp.full((distance * tokens,), -1, jnp.int32), doc_ids), 0)
    window = lax.dynamic_slice_in_dim(padded, base, (distance + 1) * tokens, 0)
    mine = lax.dynamic_slice_in_dim(doc_ids, base, tokens, 0)
    starts = base - distance * tokens + jnp.sum(
        (window[:, None] < mine[None, :]).astype(jnp.int32), 0, dtype=jnp.int32
    )
    tiles = starts.reshape(-1, TILE)
    scalars = jnp.concatenate(
        (base[None].astype(jnp.int32), jnp.stack((tiles[:, 0], tiles[:, -1]), 1).reshape(-1))
    )
    span = share * TILE
    all_tiles = (distance + 1) * tokens // TILE
    attended, grad_query, part = pl.pallas_call(
        functools.partial(attend_kernel, distance, HD ** -0.5),
        out_shape=(
            jax.ShapeDtypeStruct((tokens, share * HD), bf16),
            jax.ShapeDtypeStruct((tokens, share * HD), bf16),
            jax.ShapeDtypeStruct((distance + 1, 2, tokens, HD), bf16),
        ),
        in_specs=[smem, vmem, vmem, vmem, vmem],
        out_specs=(vmem,) * 3,
        scratch_shapes=[
            pltpu.VMEM((2, (distance + 1) * tokens, HD), f32),
            pltpu.VMEM((DOC_MOST // TILE + 1, TILE, span), f32),
            pltpu.VMEM((span, HD), bf16),
            pltpu.VMEM((HD, span), bf16),
            pltpu.VMEM((span, HD), bf16),
            pltpu.VMEM((HD, span), bf16),
            pltpu.VMEM((8, span), f32),
            pltpu.VMEM((8, span), f32),
            pltpu.VMEM((HD, span), f32),
            pltpu.VMEM((HD, span), f32),
            pltpu.VMEM((all_tiles, HD, TILE), bf16),
            pltpu.VMEM((all_tiles, HD, TILE), bf16),
        ],
        compiler_params=pltpu.CompilerParams(vmem_limit_bytes=limit),
        name="attend",
    )(scalars, starts[None, :], q_all, g_all, band)

    return pl.pallas_call(
        functools.partial(return_kernel, heads, ctx_low, blocks, distance),
        out_shape=(
            jax.ShapeDtypeStruct(queries.shape, bf16),
            jax.ShapeDtypeStruct(queries.shape, bf16),
            jax.ShapeDtypeStruct(keys.shape, bf16),
            jax.ShapeDtypeStruct(keys.shape, bf16),
        ),
        in_specs=[vmem] * 3,
        out_specs=(vmem,) * 4,
        scratch_shapes=[
            pltpu.VMEM((distance, 2, tokens, HD), bf16),
            pltpu.VMEM((distance, 2, tokens, HD), bf16),
            dma((4,)), dma((4, group - 1)), dma((4, group - 1)),
            dma((distance, 2)), dma((distance, 2)),
        ],
        compiler_params=pltpu.CompilerParams(
            collective_id=2, has_side_effects=True, vmem_limit_bytes=limit
        ),
        name="give_back",
    )(attended, grad_query, part)


def solution(mesh):
    spec = P(("ctx", "head"), None)
    return jax.shard_map(
        per_device,
        mesh=mesh,
        in_specs=(spec, spec, spec, spec, P()),
        out_specs=(spec, spec, spec, spec),
        check_vma=False,
    )
```

time: 587 us -> 135 us (0.23)
  matrix products: 209 us -> 0 us
  waiting for transfers between devices: 194 us -> 0 us
  Pallas kernels: 0 us -> 125 us
  starting transfers between devices: 68.8 us -> 0 us
  other arithmetic: 43.9 us -> 2.13 us
  blocking collectives: 31.3 us -> 0 us
  local copies, waits for them, and re-layouts: 34 us -> 6.34 us
    dot_general x96 -> x0, matrix products: 209 us -> none  [the longest x16 47.2 us: one_head(): lax.dot_general(weights, grad_head, (((0,), (0,)), ((), ())), preferred_e...]
    ppermute x16 -> x0, waiting for transfers between devices: 174 us -> none  [shifted(): return lax.ppermute(value, axis, pairs)]
    pallas_call x0 -> x3, Pallas kernels: none -> 125 us  [the longest x1 63.5 us: per_device(): pl.pallas_call(functools.partial(return_kernel, heads, ctx_low, blocks, d...]
    ppermute x16 -> x0, starting transfers between devices: 50.2 us -> none  [shifted(): return lax.ppermute(value, axis, pairs)]
    all_to_all x3 -> x0, blocking collectives: 31.3 us -> none  [the longest x1 14.4 us: per_device(): lax.all_to_all(attended, 'head', split_axis=0, concat_axis=1, tiled=True)]
    all_to_all x5 -> x0, waiting for transfers between devices: 20.1 us -> none  [the longest x1 7.88 us: per_device(): lax.all_to_all(grad_out, 'head', split_axis=1, concat_axis=0, tiled=True)]
    all_to_all x5 -> x0, starting transfers between devices: 18.6 us -> none  [the longest x1 4.4 us: per_device(): lax.all_to_all(queries, 'head', split_axis=1, concat_axis=0, tiled=True)]
    reduce_sum x16 -> x1, other arithmetic: 17.4 us -> 1.45 us  [per_device(): jnp.sum((window[:, None] < mine[None, :]).astype(jnp.int32), 0, dtype=jnp...]
  transfers between devices with their start and end apart: 21 -> 0, of which waited for: 20 -> 0; matrix products, arithmetic and copies ran while one was open for 4% -> 0% of each run, Pallas kernels for 0% -> 0%
where the time goes in v1:
time: 135 us; the launch traced here: 134 us
  Pallas kernels  125 us (93%)
  local copies, waits for them, and re-layouts  6.34 us (5%)
  other arithmetic  2.13 us (2%)
    pallas_call x1, Pallas kernels, per_device(): pl.pallas_call(functools.partial(return_kernel, heads, ctx_low, blocks, d...  63.5 us
    pallas_call x1, Pallas kernels, per_device(): pl.pallas_call(functools.partial(gather_kernel, heads, ctx_low, blocks, d...  36.3 us
    pallas_call x1, Pallas kernels, per_device(): pl.pallas_call(functools.partial(attend_kernel, distance, HD ** (-0.5)),...  25.4 us
    unnamed x12, local copies, waits for them, and re-layouts  4.78 us

profile of v1, /device:TPU:8, one launch (start us, length us, event | category | flops | bytes accessed | tf_op | source)
XLA Modules:
  0.0 134.5 jit_solution(3517030037926850330)
XLA Ops:
  0.7 0.7 dynamic_slice.7
  1.3 0.7 pad_dynamic-slice_fusion
  2.0 1.5 %convert_reduce_fusion = s32[1024]{0:T(1024)S(1)} fusion(s32[1024]{0:T(1024)S(1)} %dynamic_slice.7, s32[3072]{0:T(1024)S(1)} %pad_dynamic-slice_fusion), kind=kLoop, calls=%fused_computation | loop fusion | flops 9436160 | bytes 20480 | tf_op jit(solution)/shard_map/reduce_sum | solution.py:375
  3.5 0.0 copy-start.3
  3.5 0.1 fusion
  3.6 0.1 pad_add_fusion
  3.7 0.1 reshape.26
  3.8 0.6 pad_add_fusion.1.sc_ref
  4.4 36.3 %gather.1 = (bf16[1024,512]{1,0:T(8,128)(2,1)}, bf16[1024,512]{1,0:T(8,128)(2,1)}, bf16[3,2,1024,128]{3,2,1,0:T(8,128)(2,1)}) custom-call(bf16[128,4096]{1,0:T(8,128)(2,1)} %q_ref.1, bf16[128,1024]{1,0:T(8,128)(2,1)} %k_ref.1, bf16[128,1024]{1,0:T(8,128)(2,1)} %v_ref.1, bf16[128,4096]{1,0:T(8,128)(2,1)} %g_ref.1), custom_call_target="tpu_custom_call" | custom-call | tf_op jit(solution)/shard_map/gather/pallas_call | solution.py:351
  40.7 0.0 copy-done.3
  40.7 25.4 %attend.1 = (bf16[1024,512]{1,0:T(8,128)(2,1)}, bf16[1024,512]{1,0:T(8,128)(2,1)}, bf16[3,2,1024,128]{3,2,1,0:T(8,128)(2,1)}) custom-call(s32[9]{0:T(128)} %pad_add_fusion.1.sc_ref, s32[1,1024]{1,0:T(1,128)} %bitcast.2, bf16[1024,512]{1,0:T(8,128)(2,1)} %get-tuple-element.10.q_ref, bf16[1024,512]{1,0:T(8,128)(2,1)} %get-tuple-element.11.g_ref, ...), custom_call_target="tpu_custom_call" | custom-call | tf_op jit(solution)/shard_map/attend/pallas_call | solution.py:384
  66.1 63.5 %give_back.1 = (bf16[128,4096]{1,0:T(8,128)(2,1)}, bf16[128,4096]{1,0:T(8,128)(2,1)}, bf16[128,1024]{1,0:T(8,128)(2,1)}, bf16[128,1024]{1,0:T(8,128)(2,1)}) custom-call(bf16[1024,512]{1,0:T(8,128)(2,1)} %get-tuple-element.13.a_ref, bf16[1024,512]{1,0:T(8,128)(2,1)} %get-tuple-element.14.d_ref, bf16[3,2,1024,128]{3,2,1,0:T(8,128)(2,1)} %get-tuple-element.15.part_ref), custom_call_target="tpu_custom_call" | custom-call | tf_op jit(solution)/shard_map/give_back/pallas_call | solution.py:411
  129.7 0.0 copy-start
  129.7 0.0 copy-start.2
  129.7 2.4 %copy.13 = bf16[128,4096]{1,0:T(8,128)(2,1)} copy(bf16[128,4096]{1,0:T(8,128)(2,1)} %get-tuple-element.22) | data formatting | bytes 2097152
  132.1 0.0 copy-done
  132.1 0.0 copy-start.1
  132.1 1.0 copy.14
  133.1 0.0 copy-done.2
  133.1 0.7 copy.15
  133.8 0.0 copy-done.1
  133.8 0.7 copy.16
  (2 shorter events, 0.0 us)
Async XLA Ops:
  3.5 37.1 %copy-start.3 = (s32[1024]{0:T(1024)}, s32[1024]{0:T(1024)S(1)}, u32[]{:S(2)}) copy-start(s32[1024]{0:T(1024)S(1)} %broadcast_add_fusion) | copy-start | bytes 12292
  129.7 2.4 %copy-start = (bf16[128,4096]{1,0:T(8,128)(2,1)S(1)}, bf16[128,4096]{1,0:T(8,128)(2,1)}, u32[]{:S(2)}) copy-start(bf16[128,4096]{1,0:T(8,128)(2,1)} %get-tuple-element.23) | copy-start | bytes 3145732
  129.7 3.4 %copy-start.2 = (bf16[128,1024]{1,0:T(8,128)(2,1)S(1)}, bf16[128,1024]{1,0:T(8,128)(2,1)}, u32[]{:S(2)}) copy-start(bf16[128,1024]{1,0:T(8,128)(2,1)} %get-tuple-element.24) | copy-start | bytes 786436
  132.1 1.7 %copy-start.1 = (bf16[128,1024]{1,0:T(8,128)(2,1)S(1)}, bf16[128,1024]{1,0:T(8,128)(2,1)}, u32[]{:S(2)}) copy-start(bf16[128,1024]{1,0:T(8,128)(2,1)} %get-tuple-element.25) | copy-start | bytes 786436

commit v2 on v0

v2 whole, which is shorter than its diff:
```python
import functools

import jax
import jax.numpy as jnp
from jax import lax
from jax.experimental import pallas as pl
from jax.experimental.pallas import tpu as pltpu
from jax.sharding import PartitionSpec as P

HD = 128
DOC_MOST = 2048
TILE = 256
LOG2E = 1.4426950408889634
MESH = pl.DeviceIdType.MESH


def place(ctx_low, heads):
    ctx, head = lax.axis_index("ctx"), lax.axis_index("head")
    block = ctx // ctx_low
    me = (ctx - block * ctx_low) * heads + head

    def member(number):
        return (block * ctx_low + number // heads, lax.rem(number, heads))

    return ctx, head, block, me, member


def greet(members, ctx, head, ctx_low, has_prev, has_next):
    barrier = pltpu.get_barrier_semaphore()
    for device in members:
        pl.semaphore_signal(barrier, inc=1, device_id=device, device_id_type=MESH)

    @pl.when(has_prev)
    def _():
        pl.semaphore_signal(barrier, inc=1, device_id=(ctx - ctx_low, head), device_id_type=MESH)

    @pl.when(has_next)
    def _():
        pl.semaphore_signal(barrier, inc=1, device_id=(ctx + ctx_low, head), device_id_type=MESH)

    near = has_prev.astype(jnp.int32) + has_next.astype(jnp.int32)
    pl.semaphore_wait(barrier, len(members) + near)


def fused_kernel(
    heads, ctx_low, blocks, distance, scale,
    start_ref, q_in, k_in, v_in, g_in,
    ao_ref, do_ref, ko_ref, vo_ref,
    qo, go, band, acc, kept, qt, gt, peak, total, ot, dqt, kt, vt, inv, delta,
    att, dq, sums, landed,
    own_sem, send_sem, recv_sem, in_send, in_recv, out_send, out_recv,
):
    group = ctx_low * heads
    rows = q_in.shape[0]
    q_cols = q_in.shape[1] // group
    tokens = qo.shape[0]
    share = q_cols // HD
    factor = scale * LOG2E
    per_block = tokens // TILE
    reach = distance * per_block + 1
    ctx, head, block, me, member = place(ctx_low, heads)
    has_prev, has_next = block > 0, block < blocks - 1
    others = [lax.rem(me + step, group) for step in range(1, group)]
    greet([member(o) for o in others], ctx, head, ctx_low, has_prev, has_next)
    mine = pl.ds(pl.multiple_of(me * rows, rows), rows)
    base = block * tokens
    first_token = base - distance * tokens
    first_kb = jnp.maximum(distance - block, 0) * per_block

    def columns(width, number):
        return pl.ds(pl.multiple_of(number * width, width), width)

    def swap(a, pick_src, pick_dst):
        local = pltpu.make_async_copy(pick_src(me), pick_dst(me), own_sem.at[a])
        local.start()
        line = []
        for step, other in enumerate(others):
            copy = pltpu.make_async_remote_copy(
                src_ref=pick_src(other), dst_ref=pick_dst(me),
                send_sem=send_sem.at[a, step], recv_sem=recv_sem.at[a, step],
                device_id=member(other), device_id_type=MESH,
            )
            copy.start()
            line.append(copy)
        return local, line

    def swap_in(a, src, width, dst):
        return swap(a, lambda n: src.at[:, columns(width, n)], lambda n: dst.at[mine])

    def swap_out(a, src, width, dst):
        return swap(
            a,
            lambda n: src.at[pl.ds(pl.multiple_of(n * rows, rows), rows)],
            lambda n: dst.at[:, columns(width, n)],
        )

    def settle(pair):
        pair[0].wait()
        for copy in pair[1]:
            copy.wait_recv()

    def hop_in(step, c):
        return pltpu.make_async_remote_copy(
            src_ref=band.at[distance - step, c], dst_ref=band.at[distance - step - 1, c],
            send_sem=in_send.at[step, c], recv_sem=in_recv.at[step, c],
            device_id=(ctx + ctx_low, head), device_id_type=MESH,
        )

    def hop_out(step, c):
        return pltpu.make_async_remote_copy(
            src_ref=sums.at[step, c], dst_ref=landed.at[step, c],
            send_sem=out_send.at[step, c], recv_sem=out_recv.at[step, c],
            device_id=(ctx - ctx_low, head), device_id_type=MESH,
        )

    kv_swap = [
        swap_in(0, k_in, HD, band.at[distance, 0]),
        swap_in(1, v_in, HD, band.at[distance, 1]),
    ]
    qg_swap = [swap_in(2, q_in, q_cols, qo), swap_in(3, g_in, q_cols, go)]
    acc[...] = jnp.zeros_like(acc)
    dqt[...] = jnp.zeros_like(dqt)
    peak[...] = jnp.full_like(peak, -1e30)
    for c in range(2):
        settle(kv_swap[c])

        @pl.when(has_next)
        def _():
            hop_in(0, c).start()

    for pair in qg_swap:
        settle(pair)

    spans = [slice(h * TILE, (h + 1) * TILE) for h in range(share)]
    cols = [slice(h * HD, (h + 1) * HD) for h in range(share)]

    def tile_rows(i):
        return pl.ds(pl.multiple_of(i * TILE, TILE), TILE)

    def turn_rows(i, _):
        here = tile_rows(i)
        for h in range(share):
            qt[i, :, spans[h]] = qo[here, cols[h]].T
            gt[i, :, spans[h]] = go[here, cols[h]].T
        return 0

    lax.fori_loop(0, per_block, turn_rows, 0)

    def fold(x, op):
        return op(x.reshape(TILE // 8, 8, TILE), 0)

    def score_slot(n, _):
        slot = distance - n

        @pl.when(block - n >= 0)
        def _():
            for c in range(2):
                @pl.when(n > 0)
                def _():
                    hop_in(n - 1, c).wait_recv()

                @pl.when((n > 0) & (n < distance) & has_next)
                def _():
                    hop_in(n, c).start()

            def key_step(t, _):
                kb = slot * per_block + t
                here = tile_rows(t)
                keys = band[slot, 0, here, :]
                kt[kb] = keys.T
                vt[kb] = band[slot, 1, here, :].T
                tile_token = first_token + kb * TILE
                col = tile_token + lax.broadcasted_iota(jnp.int32, (TILE, TILE), 0)

                def row_step(i, _):
                    starts = start_ref[i]
                    token = base + i * TILE + lax.broadcasted_iota(jnp.int32, (TILE, TILE), 1)
                    seen = (col >= starts) & (col <= token)
                    for h in range(share):
                        s = jnp.dot(keys, qt[i, :, spans[h]], preferred_element_type=jnp.float32)
                        s = jnp.where(seen, s, -1e30)
                        kept[i, kb - i, :, spans[h]] = s
                        peak[i, :, spans[h]] = jnp.maximum(peak[i, :, spans[h]], fold(s, jnp.max))
                    return 0

                lax.fori_loop(
                    jnp.maximum(kb - reach + 1, 0), jnp.minimum(kb + 1, per_block), row_step, 0
                )
                return 0

            lax.fori_loop(0, per_block, key_step, 0)

        return 0

    lax.fori_loop(0, distance + 1, score_slot, 0)

    def forward_tile(i, _):
        here = tile_rows(i)
        top = jnp.max(peak[i], 0, keepdims=True) * factor
        total[...] = jnp.zeros_like(total)
        ot[...] = jnp.zeros_like(ot)

        def forward(kb, _):
            values_t = vt[kb]
            for h in range(share):
                span = spans[h]
                p = jnp.exp2(kept[i, kb - i, :, span] * factor - top[:, span])
                kept[i, kb - i, :, span] = p
                total[:, span] += fold(p, jnp.sum)
                ot[:, span] += jnp.dot(
                    values_t, p.astype(jnp.bfloat16), preferred_element_type=jnp.float32
                )
            return 0

        lax.fori_loop(jnp.maximum(i, first_kb), i + reach, forward, 0)
        inverse = 1.0 / jnp.sum(total[...], 0, keepdims=True)
        out = ot[...] * inverse
        inv[i] = inverse
        delta[i] = jnp.sum(out * gt[i].astype(jnp.float32), 0, keepdims=True)
        for h in range(share):
            att[here, cols[h]] = out[:, spans[h]].T.astype(jnp.bfloat16)
        return 0

    lax.fori_loop(0, per_block, forward_tile, 0)
    att_swap = swap_out(4, att, q_cols, ao_ref)

    def back_slot(slot, _):
        @pl.when(block - (distance - slot) >= 0)
        def _():
            def key_step(t, _):
                kb = slot * per_block + t
                values = band[slot, 1, tile_rows(t), :]
                keys_t = kt[kb]

                def row_step(i, _):
                    here = tile_rows(i)
                    dv = jnp.zeros((TILE, HD), jnp.float32)
                    dk = jnp.zeros((TILE, HD), jnp.float32)
                    inverse, shift = inv[i], delta[i]
                    for h in range(share):
                        span = spans[h]
                        w = kept[i, kb - i, :, span] * inverse[:, span]
                        dp = jnp.dot(values, gt[i, :, span], preferred_element_type=jnp.float32)
                        ds = (w * (dp - shift[:, span])).astype(jnp.bfloat16)
                        dv += jnp.dot(
                            w.astype(jnp.bfloat16), go[here, cols[h]],
                            preferred_element_type=jnp.float32,
                        )
                        dk += jnp.dot(ds, qo[here, cols[h]], preferred_element_type=jnp.float32)
                        dqt[i, :, span] += jnp.dot(keys_t, ds, preferred_element_type=jnp.float32)
                    acc[0, tile_rows(kb), :] += dk
                    acc[1, tile_rows(kb), :] += dv
                    return 0

                lax.fori_loop(
                    jnp.maximum(kb - reach + 1, 0), jnp.minimum(kb + 1, per_block), row_step, 0
                )
                return 0

            lax.fori_loop(0, per_block, key_step, 0)
            whole = pl.ds(pl.multiple_of(slot * tokens, tokens), tokens)
            for c in range(2):
                by = scale if c == 0 else 1.0

                @pl.when((slot > 0) & has_next)
                def _():
                    hop_out(slot - 1, c).wait_recv()
                    both = acc[c, whole, :] * by + landed[slot - 1, c].astype(jnp.float32)
                    sums[slot, c] = both.astype(jnp.bfloat16)

                @pl.when(jnp.logical_not((slot > 0) & has_next))
                def _():
                    sums[slot, c] = (acc[c, whole, :] * by).astype(jnp.bfloat16)

            for c in range(2):
                @pl.when(slot < distance)
                def _():
                    hop_out(slot, c).start()

        return 0

    lax.fori_loop(0, distance + 1, back_slot, 0)

    def turn_back(i, _):
        for h in range(share):
            dq[tile_rows(i), cols[h]] = (dqt[i, :, spans[h]] * scale).T.astype(jnp.bfloat16)
        return 0

    lax.fori_loop(0, per_block, turn_back, 0)
    out_swaps = [
        swap_out(5, dq, q_cols, do_ref),
        swap_out(6, sums.at[distance, 0], HD, ko_ref),
        swap_out(7, sums.at[distance, 1], HD, vo_ref),
    ]
    for pair in kv_swap + qg_swap:
        for copy in pair[1]:
            copy.wait_send()
    for pair in [att_swap] + out_swaps:
        settle(pair)
        for copy in pair[1]:
            copy.wait_send()
    for c in range(2):
        for step in range(distance):
            @pl.when((block - step >= 0) & has_next)
            def _():
                hop_in(step, c).wait_send()

            @pl.when(block - (distance - step) >= 0)
            def _():
                hop_out(step, c).wait_send()


def per_device(queries, keys, values, grad_out, doc_ids):
    heads = lax.axis_size("head")
    peers = lax.axis_size("ctx")
    rows = queries.shape[0]
    group = keys.shape[1] // HD
    share = queries.shape[1] // HD // group
    ctx_low = group // heads
    blocks = peers // ctx_low
    tokens = rows * group
    distance = DOC_MOST // tokens
    bf16, f32 = jnp.bfloat16, jnp.float32
    vmem = pl.BlockSpec(memory_space=pltpu.VMEM)
    hbm = pl.BlockSpec(memory_space=pl.ANY)
    dma = pltpu.SemaphoreType.DMA
    base = lax.axis_index("ctx") // ctx_low * tokens
    padded = jnp.concatenate((jnp.full((distance * tokens,), -1, jnp.int32), doc_ids), 0)
    window = lax.dynamic_slice_in_dim(padded, base, (distance + 1) * tokens, 0)
    mine = lax.dynamic_slice_in_dim(doc_ids, base, tokens, 0)
    starts = base - distance * tokens + jnp.sum(
        (window[:, None] < mine[None, :]).astype(jnp.int32), 0, dtype=jnp.int32
    )
    tiles = tokens // TILE
    span = share * TILE
    all_tiles = (distance + 1) * tiles
    return pl.pallas_call(
        functools.partial(fused_kernel, heads, ctx_low, blocks, distance, HD ** -0.5),
        out_shape=(
            jax.ShapeDtypeStruct(queries.shape, bf16),
            jax.ShapeDtypeStruct(queries.shape, bf16),
            jax.ShapeDtypeStruct(keys.shape, bf16),
            jax.ShapeDtypeStruct(keys.shape, bf16),
        ),
        in_specs=[vmem] + [hbm] * 4,
        out_specs=(hbm,) * 4,
        scratch_shapes=[
            pltpu.VMEM((tokens, share * HD), bf16),
            pltpu.VMEM((tokens, share * HD), bf16),
            pltpu.VMEM((distance + 1, 2, tokens, HD), bf16),
            pltpu.VMEM((2, (distance + 1) * tokens, HD), f32),
            pltpu.VMEM((tiles, distance * tiles + 1, TILE, span), f32),
            pltpu.VMEM((tiles, HD, span), bf16),
            pltpu.VMEM((tiles, HD, span), bf16),
            pltpu.VMEM((tiles, 8, span), f32),
            pltpu.VMEM((8, span), f32),
            pltpu.VMEM((HD, span), f32),
            pltpu.VMEM((tiles, HD, span), f32),
            pltpu.VMEM((all_tiles, HD, TILE), bf16),
            pltpu.VMEM((all_tiles, HD, TILE), bf16),
            pltpu.VMEM((tiles, 1, span), f32),
            pltpu.VMEM((tiles, 1, span), f32),
            pltpu.VMEM((tokens, share * HD), bf16),
            pltpu.VMEM((tokens, share * HD), bf16),
            pltpu.VMEM((distance + 1, 2, tokens, HD), bf16),
            pltpu.VMEM((distance, 2, tokens, HD), bf16),
            dma((8,)), dma((8, group - 1)), dma((8, group - 1)),
            dma((distance, 2)), dma((distance, 2)), dma((distance, 2)), dma((distance, 2)),
        ],
        compiler_params=pltpu.CompilerParams(
            collective_id=1, has_side_effects=True, vmem_limit_bytes=67043328
        ),
        name="fused",
    )(starts.reshape(tiles, 1, TILE), queries, keys, values, grad_out)


def solution(mesh):
    spec = P(("ctx", "head"), None)
    return jax.shard_map(
        per_device,
        mesh=mesh,
        in_specs=(spec, spec, spec, spec, P()),
        out_specs=(spec, spec, spec, spec),
        check_vma=False,
    )
```

time: 587 us -> 137 us (0.23)
  matrix products: 209 us -> 0 us
  waiting for transfers between devices: 194 us -> 0 us
  Pallas kernels: 0 us -> 127 us
  starting transfers between devices: 68.8 us -> 0 us
  other arithmetic: 43.9 us -> 2.05 us
  blocking collectives: 31.3 us -> 0 us
  local copies, waits for them, and re-layouts: 34 us -> 6.27 us
    dot_general x96 -> x0, matrix products: 209 us -> none  [the longest x16 47.2 us: one_head(): lax.dot_general(weights, grad_head, (((0,), (0,)), ((), ())), preferred_e...]
    ppermute x16 -> x0, waiting for transfers between devices: 174 us -> none  [shifted(): return lax.ppermute(value, axis, pairs)]
    pallas_call x0 -> x1, Pallas kernels: none -> 127 us  [per_device(): pl.pallas_call(functools.partial(fused_kernel, heads, ctx_low, blocks, di...]
    ppermute x16 -> x0, starting transfers between devices: 50.2 us -> none  [shifted(): return lax.ppermute(value, axis, pairs)]
    all_to_all x3 -> x0, blocking collectives: 31.3 us -> none  [the longest x1 14.4 us: per_device(): lax.all_to_all(attended, 'head', split_axis=0, concat_axis=1, tiled=True)]
    all_to_all x5 -> x0, waiting for transfers between devices: 20.1 us -> none  [the longest x1 7.88 us: per_device(): lax.all_to_all(grad_out, 'head', split_axis=1, concat_axis=0, tiled=True)]
    all_to_all x5 -> x0, starting transfers between devices: 18.6 us -> none  [the longest x1 4.4 us: per_device(): lax.all_to_all(queries, 'head', split_axis=1, concat_axis=0, tiled=True)]
    reduce_sum x16 -> x1, other arithmetic: 17.4 us -> 1.45 us  [per_device(): jnp.sum((window[:, None] < mine[None, :]).astype(jnp.int32), 0, dtype=jnp...]
  transfers between devices with their start and end apart: 21 -> 0, of which waited for: 20 -> 0; matrix products, arithmetic and copies ran while one was open for 4% -> 0% of each run, Pallas kernels for 0% -> 0%
where the time goes in v2:
time: 137 us; the launch traced here: 136 us
  Pallas kernels  127 us (93%)
  local copies, waits for them, and re-layouts  6.27 us (5%)
  other arithmetic  2.05 us (1%)
    pallas_call x1, Pallas kernels, per_device(): pl.pallas_call(functools.partial(fused_kernel, heads, ctx_low, blocks, di...  127 us
    unnamed x10, local copies, waits for them, and re-layouts  4.88 us

profile of v2, /device:TPU:8, one launch (start us, length us, event | category | flops | bytes accessed | tf_op | source)
XLA Modules:
  0.0 136.0 jit_solution(11228239484942420081)
XLA Ops:
  0.7 0.7 dynamic_slice.7
  1.3 0.7 pad_dynamic-slice_fusion
  2.0 1.5 %convert_reduce_fusion = s32[1024]{0:T(1024)S(1)} fusion(s32[1024]{0:T(1024)S(1)} %dynamic_slice.7, s32[3072]{0:T(1024)S(1)} %pad_dynamic-slice_fusion), kind=kLoop, calls=%fused_computation | loop fusion | flops 9436160 | bytes 20480 | tf_op jit(solution)/shard_map/reduce_sum | solution.py:331
  3.5 0.6 broadcast_add_fusion
  4.1 127.0 %fused.1 = (bf16[128,4096]{1,0:T(8,128)(2,1)}, bf16[128,4096]{1,0:T(8,128)(2,1)}, bf16[128,1024]{1,0:T(8,128)(2,1)}, bf16[128,1024]{1,0:T(8,128)(2,1)}) custom-call(s32[4,1,256]{2,1,0:T(1,128)} %bitcast.1, bf16[128,4096]{1,0:T(8,128)(2,1)} %q_in.1, bf16[128,1024]{1,0:T(8,128)(2,1)} %k_in.1, bf16[128,1024]{1,0:T(8,128)(2,1)} %v_in.1, bf16[128,4096]{1,0:T(8,128)(2,1)} %g_in.1), custom_call_target="tpu_custom_call" | custom-call | tf_op jit(solution)/shard_map/fused/pallas_call | solution.py:337
  131.1 0.0 copy-start
  131.1 2.4 %copy.13 = bf16[128,4096]{1,0:T(8,128)(2,1)} copy(bf16[128,4096]{1,0:T(8,128)(2,1)} %get-tuple-element.8) | data formatting | bytes 2097152
  133.5 0.0 copy-done
  133.5 0.0 copy-start.2
  133.5 0.0 copy-start.1
  133.5 1.0 copy.14
  134.5 0.1 copy-done.2
  134.6 0.7 copy.15
  135.3 0.0 copy-done.1
  135.3 0.7 copy.16
Async XLA Ops:
  131.1 2.4 %copy-start = (bf16[128,4096]{1,0:T(8,128)(2,1)S(1)}, bf16[128,4096]{1,0:T(8,128)(2,1)}, u32[]{:S(2)}) copy-start(bf16[128,4096]{1,0:T(8,128)(2,1)} %get-tuple-element.9) | copy-start | bytes 3145732
  133.5 1.1 copy-start.2
  133.5 1.8 %copy-start.1 = (bf16[128,1024]{1,0:T(8,128)(2,1)S(1)}, bf16[128,1024]{1,0:T(8,128)(2,1)}, u32[]{:S(2)}) copy-start(bf16[128,1024]{1,0:T(8,128)(2,1)} %get-tuple-element.11) | copy-start | bytes 786436

commit v3 on v2

--- a/solution.py
+++ b/solution.py
@@ -47,7 +47,7 @@
     start_ref, q_in, k_in, v_in, g_in,
     ao_ref, do_ref, ko_ref, vo_ref,
     qo, go, band, acc, kept, qt, gt, peak, total, ot, dqt, kt, vt, inv, delta,
-    att, dq, sums, landed,
+    att, dq, sums, landed, wide,
     own_sem, send_sem, recv_sem, in_send, in_recv, out_send, out_recv,
 ):
     group = ctx_low * heads
@@ -146,6 +146,11 @@
 
     lax.fori_loop(0, per_block, turn_rows, 0)
 
+    def across(x, y):
+        return lax.dot_general(
+            x, y, (((1,), (1,)), ((), ())), preferred_element_type=jnp.float32
+        )
+
     def fold(x, op):
         return op(x.reshape(TILE // 8, 8, TILE), 0)
 
@@ -233,23 +238,18 @@
                 keys_t = kt[kb]
 
                 def row_step(i, _):
-                    here = tile_rows(i)
-                    dv = jnp.zeros((TILE, HD), jnp.float32)
-                    dk = jnp.zeros((TILE, HD), jnp.float32)
                     inverse, shift = inv[i], delta[i]
                     for h in range(share):
                         span = spans[h]
                         w = kept[i, kb - i, :, span] * inverse[:, span]
                         dp = jnp.dot(values, gt[i, :, span], preferred_element_type=jnp.float32)
-                        ds = (w * (dp - shift[:, span])).astype(jnp.bfloat16)
-                        dv += jnp.dot(
-                            w.astype(jnp.bfloat16), go[here, cols[h]],
-                            preferred_element_type=jnp.float32,
-                        )
-                        dk += jnp.dot(ds, qo[here, cols[h]], preferred_element_type=jnp.float32)
-                        dqt[i, :, span] += jnp.dot(keys_t, ds, preferred_element_type=jnp.float32)
-                    acc[0, tile_rows(kb), :] += dk
-                    acc[1, tile_rows(kb), :] += dv
+                        wide[0, :, span] = w.astype(jnp.bfloat16)
+                        wide[1, :, span] = (w * (dp - shift[:, span])).astype(jnp.bfloat16)
+                    dqt[i] += jnp.dot(keys_t, wide[1], preferred_element_type=jnp.float32)
+                    dv = across(gt[i], wide[0])
+                    dk = across(qt[i], wide[1])
+                    acc[0, kb] += dk
+                    acc[1, kb] += dv
                     return 0
 
                 lax.fori_loop(
@@ -258,19 +258,24 @@
                 return 0
 
             lax.fori_loop(0, per_block, key_step, 0)
-            whole = pl.ds(pl.multiple_of(slot * tokens, tokens), tokens)
             for c in range(2):
                 by = scale if c == 0 else 1.0
 
+                def term(t):
+                    return (acc[c, slot * per_block + t] * by).T
+
                 @pl.when((slot > 0) & has_next)
                 def _():
                     hop_out(slot - 1, c).wait_recv()
-                    both = acc[c, whole, :] * by + landed[slot - 1, c].astype(jnp.float32)
-                    sums[slot, c] = both.astype(jnp.bfloat16)
+                    for t in range(per_block):
+                        rows_t = slice(t * TILE, (t + 1) * TILE)
+                        both = term(t) + landed[slot - 1, c, rows_t, :].astype(jnp.float32)
+                        sums[slot, c, rows_t, :] = both.astype(jnp.bfloat16)
 
                 @pl.when(jnp.logical_not((slot > 0) & has_next))
                 def _():
-                    sums[slot, c] = (acc[c, whole, :] * by).astype(jnp.bfloat16)
+                    for t in range(per_block):
+                        sums[slot, c, t * TILE:(t + 1) * TILE, :] = term(t).astype(jnp.bfloat16)
 
             for c in range(2):
                 @pl.when(slot < distance)
@@ -348,7 +353,7 @@
             pltpu.VMEM((tokens, share * HD), bf16),
             pltpu.VMEM((tokens, share * HD), bf16),
             pltpu.VMEM((distance + 1, 2, tokens, HD), bf16),
-            pltpu.VMEM((2, (distance + 1) * tokens, HD), f32),
+            pltpu.VMEM((2, all_tiles, HD, TILE), f32),
             pltpu.VMEM((tiles, distance * tiles + 1, TILE, span), f32),
             pltpu.VMEM((tiles, HD, span), bf16),
             pltpu.VMEM((tiles, HD, span), bf16),
@@ -364,6 +369,7 @@
             pltpu.VMEM((tokens, share * HD), bf16),
             pltpu.VMEM((distance + 1, 2, tokens, HD), bf16),
             pltpu.VMEM((distance, 2, tokens, HD), bf16),
+            pltpu.VMEM((2, TILE, span), bf16),
             dma((8,)), dma((8, group - 1)), dma((8, group - 1)),
             dma((distance, 2)), dma((distance, 2)), dma((distance, 2)), dma((distance, 2)),
         ],

time: 137 us -> 132 us (0.964)
  Pallas kernels: 127 us -> 122 us
    pallas_call x1, Pallas kernels: 127 us -> 122 us  [per_device(): pl.pallas_call(functools.partial(fused_kernel, heads, ctx_low, blocks, di...]
where the time goes in v3:
time: 132 us; the launch traced here: 131 us
  Pallas kernels  122 us (92%)
  local copies, waits for them, and re-layouts  6.27 us (5%)
  other arithmetic  2.05 us (2%)
    pallas_call x1, Pallas kernels, per_device(): pl.pallas_call(functools.partial(fused_kernel, heads, ctx_low, blocks, di...  122 us
    unnamed x10, local copies, waits for them, and re-layouts  4.88 us

profile of v3, /device:TPU:8, one launch (start us, length us, event | category | flops | bytes accessed | tf_op | source)
XLA Modules:
  0.0 130.7 jit_solution(6661785699345395245)
XLA Ops:
  0.7 0.7 dynamic_slice.7
  1.3 0.7 pad_dynamic-slice_fusion
  2.0 1.5 %convert_reduce_fusion = s32[1024]{0:T(1024)S(1)} fusion(s32[1024]{0:T(1024)S(1)} %dynamic_slice.7, s32[3072]{0:T(1024)S(1)} %pad_dynamic-slice_fusion), kind=kLoop, calls=%fused_computation | loop fusion | flops 9436160 | bytes 20480 | tf_op jit(solution)/shard_map/reduce_sum | solution.py:336
  3.5 0.6 broadcast_add_fusion
  4.1 121.7 %fused.1 = (bf16[128,4096]{1,0:T(8,128)(2,1)}, bf16[128,4096]{1,0:T(8,128)(2,1)}, bf16[128,1024]{1,0:T(8,128)(2,1)}, bf16[128,1024]{1,0:T(8,128)(2,1)}) custom-call(s32[4,1,256]{2,1,0:T(1,128)} %bitcast.1, bf16[128,4096]{1,0:T(8,128)(2,1)} %q_in.1, bf16[128,1024]{1,0:T(8,128)(2,1)} %k_in.1, bf16[128,1024]{1,0:T(8,128)(2,1)} %v_in.1, bf16[128,4096]{1,0:T(8,128)(2,1)} %g_in.1), custom_call_target="tpu_custom_call" | custom-call | tf_op jit(solution)/shard_map/fused/pallas_call | solution.py:342
  125.8 0.0 copy-start
  125.8 2.4 %copy.13 = bf16[128,4096]{1,0:T(8,128)(2,1)} copy(bf16[128,4096]{1,0:T(8,128)(2,1)} %get-tuple-element.8) | data formatting | bytes 2097152
  128.2 0.0 copy-done
  128.2 0.0 copy-start.2
  128.2 0.0 copy-start.1
  128.2 1.0 copy.14
  129.1 0.1 copy-done.2
  129.3 0.7 copy.15
  130.0 0.0 copy-done.1
  130.0 0.7 copy.16
Async XLA Ops:
  125.8 2.4 %copy-start = (bf16[128,4096]{1,0:T(8,128)(2,1)S(1)}, bf16[128,4096]{1,0:T(8,128)(2,1)}, u32[]{:S(2)}) copy-start(bf16[128,4096]{1,0:T(8,128)(2,1)} %get-tuple-element.9) | copy-start | bytes 3145732
  128.2 1.1 copy-start.2
  128.2 1.8 %copy-start.1 = (bf16[128,1024]{1,0:T(8,128)(2,1)S(1)}, bf16[128,1024]{1,0:T(8,128)(2,1)}, u32[]{:S(2)}) copy-start(bf16[128,1024]{1,0:T(8,128)(2,1)} %get-tuple-element.11) | copy-start | bytes 786436
